TPU v7x, 512 devices: a whole 4x8x8 slice. The times are simulated.
512 devices in a mesh: pair: 16 (over z, core), virt: 32 (over x, y).
Axes of the slice: x: 4, y: 8, z: 8, core: 2. Of those that a mesh axis runs over, the one named last changes fastest.
Arguments:
- amplitudes: bfloat16 [1024, 512, 512], P('pair', 'virt')
- integrals: bfloat16 [8, 512, 512, 512], P(None, 'pair', 'virt')
- pair_occ: int32 [1024, 2], P('virt'), may hold values from 0 to 119, as said below
- occ_irrep: int32 [120], replicated, may hold values from 0 to 7, as said below
- virt_irrep: int32 [512], replicated, may hold values from 0 to 7, as said below
- occ_energy: float32 [120], replicated, may hold values from -3 to -0.5
- virt_energy: float32 [512], replicated, may hold values from 0.3 to 4
Outputs:
- update: float32 [1024, 8, 512], P('virt', None, 'pair')
Inputs may be any that keep to these rules, and one draw needn't show every extreme that they name: `pair_occ`: each row holds i < j, and rows are distinct. `occ_irrep`: labels of the D2h irreps; every label occurs. `virt_irrep`: labels of the D2h irreps; every label occurs.
All inputs are finite; a program needn't handle non-finite values.
Results may differ from a plain program's by a relative error of at most 0.0003.
Values may be sent and summed in bfloat16 or wider, within the bound.
A program may use at most 128 MiB of HBM per device.

v0:
```python
import jax
import jax.numpy as jnp
from jax import lax
from jax.sharding import PartitionSpec as P


def table_lookup(indices, table, zero_value):
    orbital = jnp.arange(table.shape[0], dtype=jnp.int32)
    hits = indices[:, None] == orbital[None, :]
    return jnp.sum(jnp.where(hits, table[None, :], zero_value), axis=1)


def local(amplitudes, integrals, pair_occ, occ_irrep, virt_irrep, occ_energy, virt_energy):
    window_size, local_width, local_depth, full_width = integrals.shape
    integral_matrix = integrals.reshape(window_size * local_width, local_depth * full_width)
    owned_rows = pair_occ.shape[0]
    block_rows = lax.all_gather(amplitudes, "pair", axis=0, tiled=True)
    flattened = block_rows.reshape(block_rows.shape[0], local_depth * full_width)
    partial_value = lax.dot_general(
        flattened, integral_matrix, (((1,), (1,)), ((), ())), preferred_element_type=jnp.float32
    )
    summed = lax.psum(partial_value, "virt")
    ladder = lax.dynamic_slice_in_dim(summed, lax.axis_index("virt") * owned_rows, owned_rows, 0)
    ladder = ladder.reshape(owned_rows, window_size, local_width)
    b_offset = lax.axis_index("pair") * local_width
    local_sym = lax.dynamic_slice_in_dim(virt_irrep, b_offset, local_width, 0)
    local_energy = lax.dynamic_slice_in_dim(virt_energy, b_offset, local_width, 0)
    first_occ = pair_occ[:, 0]
    second_occ = pair_occ[:, 1]
    pair_sym = jnp.bitwise_xor(
        table_lookup(first_occ, occ_irrep, 0), table_lookup(second_occ, occ_irrep, 0)
    )
    pair_energy = table_lookup(first_occ, occ_energy, 0.0) + table_lookup(
        second_occ, occ_energy, 0.0
    )
    window_sym = virt_irrep[:window_size]
    total_sym = jnp.bitwise_xor(
        pair_sym[:, None, None],
        jnp.bitwise_xor(window_sym[None, :, None], local_sym[None, None, :]),
    )
    allowed = total_sym == 0
    denom = (
        pair_energy[:, None, None]
        - virt_energy[:window_size][None, :, None]
        - local_energy[None, None, :]
    )
    return jnp.where(allowed, ladder / denom, jnp.zeros_like(ladder))


def solution(mesh):
    return jax.shard_map(
        local,
        mesh=mesh,
        in_specs=(
            P("pair", "virt", None),
            P(None, "pair", "virt", None),
            P("virt", None),
            P(),
            P(),
            P(),
            P(),
        ),
        out_specs=P("virt", None, "pair"),
        check_vma=False,
    )
```

profile of v0, /device:TPU:64, one launch (start us, length us, event | category | flops | bytes accessed | tf_op | source)
XLA Modules:
  0.0 301.6 jit_solution(1929621240613633479)
XLA Ops:
  6.5 0.0 all-gather.2.cloned.1.call-start
  6.5 0.7 all-gather.2.cloned.1.call-update
  7.3 0.0 all-reduce.2.cloned.1.call-start
  7.3 8.4 %copy.9 = bf16[32,8,16,512]{3,1,2,0:T(8,128)(2,1)} copy(bf16[32,8,16,512]{3,2,1,0:T(8,128)(2,1)} %bitcast.13) | data formatting | bytes 8388608
  15.7 94.0 %all-gather.2.cloned.1.call-done = bf16[1024,16,512]{2,1,0:T(8,128)(2,1)} async-done(((bf16[64,16,512]{2,1,0:T(8,128)(2,1)}), bf16[1024,16,512]{2,1,0:T(8,128)(2,1)}) %all-gather.2.cloned.1.call-update) | async-done | bytes 16777232 | tf_op jit(solution)/shard_map/all_gather | solution.py:17
  109.7 16.0 %copy.8 = bf16[128,8,16,512]{3,1,2,0:T(8,128)(2,1)S(1)} copy(bf16[128,8,16,512]{3,2,1,0:T(8,128)(2,1)} %bitcast.11) | data formatting | bytes 33554432
  125.7 0.0 copy-start.4
  125.7 0.0 copy-start.5
  125.7 0.0 copy-start.1
  125.8 0.0 copy-start.2
  125.8 0.0 copy-start.3
  125.8 0.0 slice-start.1
  125.8 0.0 slice-start
  125.8 0.0 copy-done
  125.8 5.5 %fusion = f32[1024,256]{1,0:T(8,128)} fusion(bf16[1024,8192]{1,0:T(8,128)(2,1)S(1)} %bitcast.12, bf16[256,8192]{1,0:T(8,128)(2,1)S(1)} %bitcast.14), kind=kOutput, calls=%fused_computation.13 | convolution fusion | flops 4294967296 | bytes 22020096 | tf_op jit(solution)/shard_map/dot_general | solution.py:19
  131.4 0.0 all-reduce.2.cloned.1.call-update
  131.4 0.0 copy-done.4
  131.4 0.1 dynamic_slice.11
  131.5 0.0 copy-done.5
  131.5 0.1 dynamic_slice.9
  131.5 0.0 copy-done.1
  131.6 0.0 copy-done.2
  131.6 0.2 select_reduce_fusion
  131.8 0.0 copy-done.3
  131.8 0.2 select_reduce_fusion.2
  132.0 0.1 broadcast_xor_fusion
  132.0 0.0 slice-done
  132.0 0.1 broadcast_subtract_fusion
  132.1 161.0 %all-reduce.2.cloned.1.call-done = f32[1024,256]{1,0:T(8,128)} async-done(((f32[1024,256]{1,0:T(8,128)}), f32[1024,256]{1,0:T(8,128)}) %all-reduce.2.cloned.1.call-update) | async-done | bytes 1048592 | tf_op jit(solution)/shard_map/psum | solution.py:22
  293.1 0.8 constant_dynamic-slice_fusion
  293.9 0.1 reshape.87
  294.0 0.8 divide_select_fusion
  (5 shorter events, 0.0 us)
Async XLA Ops:
  6.5 103.2 %all-gather.2.cloned.1.call-start = ((), (), s32[]{:S(2)}) async-start(), calls=%async_computation | async-start | bytes 17825792 | tf_op jit(solution)/shard_map/all_gather | solution.py:17
  7.3 285.9 %all-reduce.2.cloned.1.call-start = ((), (), s32[]{:S(2)}) async-start(), calls=%async_computation.1 | async-start | bytes 2097152 | tf_op jit(solution)/shard_map/psum | solution.py:22
  109.7 16.1 %copy-start = (bf16[32,8,16,512]{3,1,2,0:T(8,128)(2,1)S(1)}, bf16[32,8,16,512]{3,1,2,0:T(8,128)(2,1)}, u32[]{:S(2)}) copy-start(bf16[32,8,16,512]{3,1,2,0:T(8,128)(2,1)} %copy.9) | copy-start | bytes 12582916
  125.7 5.7 %copy-start.4 = (f32[512]{0:T(512)S(1)}, f32[512]{0:T(512)}, u32[]{:S(2)}) copy-start(f32[512]{0:T(512)} %param.13) | copy-start | bytes 6148
  125.7 5.7 %copy-start.5 = (s32[512]{0:T(512)S(1)}, s32[512]{0:T(512)}, u32[]{:S(2)}) copy-start(s32[512]{0:T(512)} %param.11) | copy-start | bytes 6148
  125.7 5.8 %copy-start.1 = (s32[32,2]{0,1:T(2,128)S(1)}, s32[32,2]{0,1:T(2,128)}, u32[]{:S(2)}) copy-start(s32[32,2]{0,1:T(2,128)} %param.9) | copy-start | bytes 772
  125.8 5.8 %copy-start.2 = (f32[120]{0:T(128)S(1)}, f32[120]{0:T(128)}, u32[]{:S(2)}) copy-start(f32[120]{0:T(128)} %param.12) | copy-start | bytes 1444
  125.8 6.0 %copy-start.3 = (s32[120]{0:T(128)S(1)}, s32[120]{0:T(128)}, u32[]{:S(2)}) copy-start(s32[120]{0:T(128)} %param.10) | copy-start | bytes 1444
  125.8 6.2 %slice-start.1 = ((s32[512]{0:T(512)}), s32[8]{0:T(128)S(1)}, s32[]{:S(2)}) async-start(s32[512]{0:T(512)} %param.11), calls=%async_computation.3 | async-start | bytes 1024 | tf_op jit(solution)/shard_map/slice | solution.py:36
  125.8 6.2 %slice-start = ((f32[512]{0:T(512)}), f32[8]{0:T(128)S(1)}, s32[]{:S(2)}) async-start(f32[512]{0:T(512)} %param.13), calls=%async_computation.2 | async-start | bytes 1024 | tf_op jit(solution)/shard_map/slice | solution.py:44
Sparse Core Ops, SparseCore 0:
  9.4 100.2 all-gather.1
  131.5 161.6 all-reduce.1
where the time goes:
time: 302 us
  waiting for transfers between devices  256 us (85%)
  local copies, waits for them, and re-layouts  25.5 us (8%)
  between operations  13.5 us (4%)
  matrix products  5.53 us (2%)
    psum x1, waiting for transfers between devices, local(): summed = lax.psum(partial_value, 'virt')  161 us
    all_gather x1, waiting for transfers between devices, local(): block_rows = lax.all_gather(amplitudes, 'pair', axis=0, tiled=True)  94 us
    unnamed x14, local copies, waits for them, and re-layouts  24.5 us
  transfers between devices with their start and end apart: 2, of which 2 were waited for; matrix products, arithmetic and copies ran while one was open for 3% of the time, Pallas kernels for 0%

commit v1 on v0

--- a/solution.py
+++ b/solution.py
@@ -19,7 +19,7 @@
     partial_value = lax.dot_general(
         flattened, integral_matrix, (((1,), (1,)), ((), ())), preferred_element_type=jnp.float32
     )
-    summed = lax.psum(partial_value, "virt")
+    summed = jnp.sum(lax.all_gather(partial_value, "virt"), 0)
     ladder = lax.dynamic_slice_in_dim(summed, lax.axis_index("virt") * owned_rows, owned_rows, 0)
     ladder = ladder.reshape(owned_rows, window_size, local_width)
     b_offset = lax.axis_index("pair") * local_width

time: 302 us -> 391 us (1.29)
  the two profiles are of different devices: /device:TPU:64 before, /device:TPU:1 now
where the time goes in v1:
time: 391 us; the launch traced here: 390 us
  waiting for transfers between devices  333 us (85%)
  local copies, waits for them, and re-layouts  24.7 us (6%)
  between operations  13.5 us (3%)
  other arithmetic  13.2 us (3%)
  matrix products  5.5 us (1%)
    all_gather x1, waiting for transfers between devices, local(): summed = jnp.sum(lax.all_gather(partial_value, 'virt'), 0)  234 us
    all_gather x1, waiting for transfers between devices, local(): block_rows = lax.all_gather(amplitudes, 'pair', axis=0, tiled=True)  98.4 us
    unnamed x14, local copies, waits for them, and re-layouts  24.5 us
    reduce_sum x1, other arithmetic, local(): summed = jnp.sum(lax.all_gather(partial_value, 'virt'), 0)  11.9 us
  transfers between devices with their start and end apart: 2, of which 2 were waited for; matrix products, arithmetic and copies ran while one was open for 2% of the time, Pallas kernels for 0%

profile of v1, /device:TPU:1, one launch (start us, length us, event | category | flops | bytes accessed | tf_op | source)
XLA Modules:
  0.0 390.4 jit_solution(478617818500520845)
XLA Ops:
  6.5 0.0 all-gather.4.cloned.1.call-start
  6.5 0.7 all-gather.4.cloned.1.call-update
  7.3 0.0 all-gather.6.cloned.1.call-start
  7.3 8.4 %copy.9 = bf16[32,8,16,512]{3,1,2,0:T(8,128)(2,1)} copy(bf16[32,8,16,512]{3,2,1,0:T(8,128)(2,1)} %bitcast.15) | data formatting | bytes 8388608
  15.7 98.4 %all-gather.4.cloned.1.call-done = bf16[1024,16,512]{2,1,0:T(8,128)(2,1)} async-done(((bf16[64,16,512]{2,1,0:T(8,128)(2,1)}), bf16[1024,16,512]{2,1,0:T(8,128)(2,1)}) %all-gather.4.cloned.1.call-update) | async-done | bytes 16777232 | tf_op jit(solution)/shard_map/all_gather | solution.py:17
  114.2 16.0 %copy.8 = bf16[128,8,16,512]{3,1,2,0:T(8,128)(2,1)S(1)} copy(bf16[128,8,16,512]{3,2,1,0:T(8,128)(2,1)} %bitcast.13) | data formatting | bytes 33554432
  130.2 0.0 copy-start.4
  130.2 0.0 copy-start.5
  130.2 0.0 copy-start.1
  130.2 0.0 copy-start.2
  130.2 0.0 copy-start.3
  130.2 0.0 slice-start.1
  130.2 0.0 slice-start
  130.2 0.0 copy-done
  130.3 5.5 %fusion = f32[1024,256]{1,0:T(8,128)} fusion(bf16[1024,8192]{1,0:T(8,128)(2,1)S(1)} %bitcast.14, bf16[256,8192]{1,0:T(8,128)(2,1)S(1)} %bitcast.16), kind=kOutput, calls=%fused_computation.13 | convolution fusion | flops 4294967296 | bytes 22020096 | tf_op jit(solution)/shard_map/dot_general | solution.py:19
  135.8 0.0 all-gather.6.cloned.1.call-update
  135.8 0.0 copy-done.4
  135.8 0.1 dynamic_slice.11
  135.9 0.0 copy-done.5
  135.9 0.1 dynamic_slice.9
  135.9 0.0 copy-done.1
  136.0 0.0 copy-done.2
  136.0 0.2 select_reduce_fusion
  136.2 0.0 copy-done.3
  136.2 0.2 select_reduce_fusion.2
  136.4 0.0 slice-done.1
  136.4 0.1 broadcast_xor_fusion
  136.4 0.1 broadcast_subtract_fusion
  136.5 234.2 %all-gather.6.cloned.1.call-done = f32[32768,256]{1,0:T(8,128)} async-done(((f32[1024,256]{1,0:T(8,128)}), f32[32768,256]{1,0:T(8,128)}) %all-gather.6.cloned.1.call-update) | async-done | bytes 33554448 | tf_op jit(solution)/shard_map/all_gather | solution.py:22
  370.7 11.9 %reduce_sum.47 = f32[1024,256]{1,0:T(8,128)S(1)} reduce(f32[32,1024,256]{2,1,0:T(8,128)} %bitcast.12, f32[]{:T(128)} %constant.6.clone.1), dimensions={0}, to_apply=%region_2.3 | reduce | flops 8126464 | bytes 34603012 | tf_op jit(solution)/shard_map/reduce_sum | solution.py:22
  382.6 0.1 reshape.87
  382.7 0.8 divide_select_fusion
  (6 shorter events, 0.0 us)
Async XLA Ops:
  6.5 107.6 %all-gather.4.cloned.1.call-start = ((), (), s32[]{:S(2)}) async-start(), calls=%async_computation | async-start | bytes 17825792 | tf_op jit(solution)/shard_map/all_gather | solution.py:17
  7.3 363.4 %all-gather.6.cloned.1.call-start = ((), (), s32[]{:S(2)}) async-start(), calls=%async_computation.1 | async-start | bytes 34603008 | tf_op jit(solution)/shard_map/all_gather | solution.py:22
  114.2 16.1 %copy-start = (bf16[32,8,16,512]{3,1,2,0:T(8,128)(2,1)S(1)}, bf16[32,8,16,512]{3,1,2,0:T(8,128)(2,1)}, u32[]{:S(2)}) copy-start(bf16[32,8,16,512]{3,1,2,0:T(8,128)(2,1)} %copy.9) | copy-start | bytes 12582916
  130.2 5.6 %copy-start.4 = (f32[512]{0:T(512)S(1)}, f32[512]{0:T(512)}, u32[]{:S(2)}) copy-start(f32[512]{0:T(512)} %param.13) | copy-start | bytes 6148
  130.2 5.7 %copy-start.5 = (s32[512]{0:T(512)S(1)}, s32[512]{0:T(512)}, u32[]{:S(2)}) copy-start(s32[512]{0:T(512)} %param.11) | copy-start | bytes 6148
  130.2 5.8 %copy-start.1 = (s32[32,2]{0,1:T(2,128)S(1)}, s32[32,2]{0,1:T(2,128)}, u32[]{:S(2)}) copy-start(s32[32,2]{0,1:T(2,128)} %param.9) | copy-start | bytes 772
  130.2 5.8 %copy-start.2 = (f32[120]{0:T(128)S(1)}, f32[120]{0:T(128)}, u32[]{:S(2)}) copy-start(f32[120]{0:T(128)} %param.12) | copy-start | bytes 1444
  130.2 5.9 %copy-start.3 = (s32[120]{0:T(128)S(1)}, s32[120]{0:T(128)}, u32[]{:S(2)}) copy-start(s32[120]{0:T(128)} %param.10) | copy-start | bytes 1444
  130.2 6.1 %slice-start.1 = ((s32[512]{0:T(512)}), s32[8]{0:T(128)S(1)}, s32[]{:S(2)}) async-start(s32[512]{0:T(512)} %param.11), calls=%async_computation.3 | async-start | bytes 1024 | tf_op jit(solution)/shard_map/slice | solution.py:36
  130.2 6.2 %slice-start = ((f32[512]{0:T(512)}), f32[8]{0:T(128)S(1)}, s32[]{:S(2)}) async-start(f32[512]{0:T(512)} %param.13), calls=%async_computation.2 | async-start | bytes 1024 | tf_op jit(solution)/shard_map/slice | solution.py:44
Sparse Core Ops, SparseCore 0:
  9.4 104.6 all-gather.3
  135.9 234.7 all-gather.5
